TPU v7x, 256 devices: a whole 4x4x8 slice. The times are simulated.
256 devices in a mesh: ctx: 64 (over y, z, core), head: 4 (over x).
Axes of the slice: x: 4, y: 4, z: 8, core: 2. Of those that a mesh axis runs over, the one named last changes fastest.
Arguments:
- query: bfloat16 [8192, 32, 128], P('ctx', 'head'), may hold values from -6 to 6
- key: bfloat16 [8192, 4, 128], P(('ctx', 'head')), may hold values from -6 to 6
- value: bfloat16 [8192, 4, 128], P(('ctx', 'head')), may hold values from -6 to 6
- d_out: bfloat16 [8192, 32, 128], P('ctx', 'head'), may hold values from -6 to 6
- seg_blocks: int32 [32], replicated, may hold values from 1 to 4, 64 in all
- seg_audio: int32 [32], replicated, may hold values 0 or 1
Outputs:
- d_query: bfloat16 [8192, 32, 128], P('ctx', 'head')
- d_key: bfloat16 [8192, 4, 128], P(('ctx', 'head'))
- d_value: bfloat16 [8192, 4, 128], P(('ctx', 'head'))
Inputs may be any that keep to these rules, and one draw needn't show every extreme that they name: `seg_blocks`: the segments tile the 64 blocks in order: their lengths sum to 64.
All inputs are finite; a program needn't handle non-finite values.
Results may differ from a plain program's by a relative error of at most 0.0055.
Values may be sent and summed in bfloat16 or wider, within the bound.
No kernel may reach another device: no remote copies, remote signals or barrier semaphores. Data moves between devices by JAX's collectives and lax.ppermute only.
A program may use at most 128 MiB of HBM per device.

v0:
```python
import math
import jax
import jax.numpy as jnp
from jax import lax
from jax.sharding import PartitionSpec as P

DH = 128
GROUP = 8
BLK = 128
NEG = -1e30


def segment_tables(seg_blocks, seg_audio, positions):
    ends = jnp.cumsum(seg_blocks)
    starts = ends - seg_blocks
    blocks = positions // BLK
    inside = (starts[None, :] <= blocks[:, None]) & (blocks[:, None] < ends[None, :])
    numbers = jnp.arange(seg_blocks.shape[0], dtype=jnp.int32)
    segment = jnp.sum(jnp.where(inside, numbers[None, :], 0), axis=1)
    audio = jnp.sum(jnp.where(inside, seg_audio[None, :], 0), axis=1)
    return (segment, audio)


def visible(query_pos, key_pos, query_seg, query_audio, key_seg):
    causal = key_pos[None, :] <= query_pos[:, None]
    span = (query_seg[:, None] == key_seg[None, :]) & (query_audio[:, None] == 1)
    return causal | span


def prepare(rows_query, rows_out, query_pos, seg_blocks, seg_audio):
    tokens = rows_query.shape[0]
    query_seg, query_audio = segment_tables(seg_blocks, seg_audio, query_pos)
    query_flat = rows_query.reshape(tokens * GROUP, DH)
    out_flat = rows_out.reshape(tokens * GROUP, DH)
    return (query_flat, out_flat, query_pos, query_seg, query_audio)


def piece_mask(group_data, keys, seg_blocks, seg_audio):
    query_flat, out_flat, query_pos, query_seg, query_audio = group_data
    key_pos = jnp.arange(keys.shape[0], dtype=jnp.int32)
    key_seg = segment_tables(seg_blocks, seg_audio, key_pos)[0]
    return visible(query_pos, key_pos, query_seg, query_audio, key_seg)


def contract_rows(left, right):
    return lax.dot_general(
        left, right, (((1,), (1,)), ((), ())), preferred_element_type=jnp.float32
    )


def contract_first(left, right):
    return lax.dot_general(
        left, right, (((0,), (0,)), ((), ())), preferred_element_type=jnp.float32
    )


def stats_group(group_data, state, piece, seg_blocks, seg_audio):
    query_flat, out_flat, query_pos, query_seg, query_audio = group_data
    keys, values = piece
    count = keys.shape[0]
    tokens = query_pos.shape[0]
    scale = 1.0 / math.sqrt(DH)
    mask = piece_mask(group_data, keys, seg_blocks, seg_audio)

    def stats_compute(kept):
        highest, total, weighted = kept
        wide = mask[:, None, :]
        scores = (contract_rows(query_flat, keys) * scale).reshape(tokens, GROUP, count)
        new_high = jnp.maximum(highest, jnp.max(jnp.where(wide, scores, NEG), axis=2))
        probs = jnp.where(wide, jnp.exp(scores - new_high[:, :, None]), 0.0)
        d_probs = contract_rows(out_flat, values).reshape(tokens, GROUP, count)
        return (new_high, jnp.sum(probs, axis=2), jnp.sum(probs * d_probs, axis=2))

    def stats_skipped(kept):
        return kept

    return lax.cond(jnp.any(mask), stats_compute, stats_skipped, state)


def grad_group(group_data, finals, grad_rows, piece, seg_blocks, seg_audio):
    query_flat, out_flat, query_pos, query_seg, query_audio = group_data
    lse, delta = finals
    keys, values = piece
    count = keys.shape[0]
    tokens = query_pos.shape[0]
    scale = 1.0 / math.sqrt(DH)
    mask = piece_mask(group_data, keys, seg_blocks, seg_audio)

    def grad_compute(grad_rows):
        wide = mask[:, None, :]
        scores = (contract_rows(query_flat, keys) * scale).reshape(tokens, GROUP, count)
        probs = jnp.where(wide, jnp.exp(scores - lse[:, :, None]), 0.0)
        d_probs = contract_rows(out_flat, values).reshape(tokens, GROUP, count)
        probs_low = probs.astype(jnp.bfloat16).reshape(tokens * GROUP, count)
        d_scores = (
            (probs * (d_probs - delta[:, :, None]))
            .astype(jnp.bfloat16)
            .reshape(tokens * GROUP, count)
        )
        value_part = contract_first(probs_low, out_flat)
        key_part = contract_first(d_scores, query_flat)
        grad_rows = jnp.dot(d_scores, keys, preferred_element_type=jnp.float32)
        return (grad_rows, key_part, value_part)

    def grad_skipped(grad_rows):
        blank = jnp.zeros((count, keys.shape[1]), jnp.float32)
        return (grad_rows, blank, blank)

    return lax.cond(jnp.any(mask), grad_compute, grad_skipped, grad_rows)


def body(query, key, value, d_out, seg_blocks, seg_audio):
    key, value = (
        lax.all_to_all(key, "head", split_axis=1, concat_axis=0, tiled=True),
        lax.all_to_all(value, "head", split_axis=1, concat_axis=0, tiled=True),
    )
    rows = query.shape[0]
    half = rows // 2
    place = lax.axis_index("ctx")
    scale = 1.0 / math.sqrt(DH)
    keys = key[:, 0, :]
    values = value[:, 0, :]
    own_pos = place * rows + jnp.arange(rows, dtype=jnp.int32)
    first = prepare(query[:half], d_out[:half], own_pos[:half], seg_blocks, seg_audio)
    second = prepare(query[half:], d_out[half:], own_pos[half:], seg_blocks, seg_audio)
    groups = (first, second)
    blank_stats = jnp.zeros((half, GROUP), jnp.float32)
    start_stats = tuple(
        (
            (jnp.full((half, GROUP), NEG, jnp.float32), blank_stats, blank_stats)
            for group_data in groups
        )
    )
    piece = (
        lax.all_gather(keys, "ctx", axis=0, tiled=True),
        lax.all_gather(values, "ctx", axis=0, tiled=True),
    )
    stats = tuple(
        (
            stats_group(group_data, state, piece, seg_blocks, seg_audio)
            for group_data, state in zip(groups, start_stats)
        )
    )
    finals = tuple(
        ((highest + jnp.log(total), weighted / total) for highest, total, weighted in stats)
    )
    blank_rows = jnp.zeros((half * GROUP, DH), jnp.float32)
    piece = (
        lax.all_gather(keys, "ctx", axis=0, tiled=True),
        lax.all_gather(values, "ctx", axis=0, tiled=True),
    )
    grad_list = (blank_rows, blank_rows)
    piece_keys = piece[0]
    count = piece_keys.shape[0]
    key_sum = jnp.zeros((count, DH), jnp.float32)
    value_sum = jnp.zeros((count, DH), jnp.float32)
    new_rows = []
    for group_data, group_finals, grad_rows in zip(groups, finals, grad_list):
        grad_rows, key_part, value_part = grad_group(
            group_data, group_finals, grad_rows, piece, seg_blocks, seg_audio
        )
        key_sum = key_sum + key_part
        value_sum = value_sum + value_part
        new_rows.append(grad_rows)
    update = jnp.stack([key_sum, value_sum], axis=1)
    key_grad = update
    grads = (key_grad, tuple(new_rows))
    key_grad, grad_list = grads
    summed = lax.psum_scatter(key_grad, "ctx", scatter_dimension=0, tiled=True)
    d_key = (summed[:, 0, :] * scale).astype(jnp.bfloat16)[:, None, :]
    d_value = summed[:, 1, :].astype(jnp.bfloat16)[:, None, :]
    first_rows = (grad_list[0] * scale).astype(jnp.bfloat16).reshape(half, GROUP, DH)
    second_rows = (grad_list[1] * scale).astype(jnp.bfloat16).reshape(half, GROUP, DH)
    d_query = jnp.concatenate([first_rows, second_rows], axis=0)
    d_key, d_value = (
        lax.all_to_all(d_key, "head", split_axis=0, concat_axis=1, tiled=True),
        lax.all_to_all(d_value, "head", split_axis=0, concat_axis=1, tiled=True),
    )
    return (d_query, d_key, d_value)


def solution(mesh):
    placed = (
        P("ctx", "head", None),
        P(("ctx", "head"), None, None),
        P(("ctx", "head"), None, None),
        P("ctx", "head", None),
        P(),
        P(),
    )
    return jax.shard_map(
        body,
        mesh=mesh,
        in_specs=placed,
        out_specs=(
            P("ctx", "head", None),
            P(("ctx", "head"), None, None),
            P(("ctx", "head"), None, None),
        ),
        check_vma=False,
    )
```

profile of v0, /device:TPU:8, one launch (start us, length us, event | category | flops | bytes accessed | tf_op | source)
XLA Modules:
  0.0 555.6 jit_solution(9331188242737443876)
XLA Ops:
  7.2 0.8 copy.34
  8.0 9.6 %all_to_all.66 = bf16[32,4,128]{2,0,1:T(8,128)(2,1)} all-to-all(bf16[32,4,128]{2,0,1:T(8,128)(2,1)S(1)} %copy.34), channel_id=1, replica_groups=mesh['ctx'=64,'head'=4] {'head'}, dimensions={1} | all-to-all | bytes 65536 | tf_op jit(solution)/shard_map/all_to_all | solution.py:114
  17.7 0.8 copy.35
  18.5 8.5 %all_to_all.67 = bf16[32,4,128]{2,0,1:T(8,128)(2,1)} all-to-all(bf16[32,4,128]{2,0,1:T(8,128)(2,1)S(1)} %copy.35), channel_id=1, replica_groups=mesh['ctx'=64,'head'=4] {'head'}, dimensions={1} | all-to-all | bytes 65536 | tf_op jit(solution)/shard_map/all_to_all | solution.py:115
  27.0 0.7 copy.33
  27.8 0.1 reduce.12
  27.9 0.7 sub.100
  28.7 0.7 select_reduce_fusion.3
  29.4 0.3 select_reduce_fusion
  29.8 2.3 fusion.16
  33.4 1.8 slice_bitcast_fusion.2
  35.2 60.1 %all-gather.3.cloned.1.call-done = bf16[8192,128]{1,0:T(8,128)(2,1)} async-done(((bf16[128,128]{1,0:T(8,128)(2,1)}), bf16[8192,128]{1,0:T(8,128)(2,1)}) %all-gather.3.cloned.1.call-update) | async-done | bytes 2097168 | tf_op jit(solution)/shard_map/all_gather | solution.py:149
  95.2 77.8 %all-gather.5.cloned.1.call-done = bf16[8192,128]{1,0:T(8,128)(2,1)} async-done(((bf16[128,128]{1,0:T(8,128)(2,1)}), bf16[8192,128]{1,0:T(8,128)(2,1)}) %all-gather.5.cloned.1.call-update) | async-done | bytes 2097168 | tf_op jit(solution)/shard_map/all_gather | solution.py:136
  173.0 30.0 %conditional.4 = (f32[64,8]{1,0:T(8,128)}, f32[64,8]{1,0:T(8,128)}, f32[64,8]{1,0:T(8,128)}) conditional(s32[]{:T(128)} %convert_element_type.36, () %tuple.57, (pred[64,8192]{1,0:T(8,128)(4,1)S(1)}, bf16[512,128]{1,0:T(8,128)(2,1)S(1)}, bf16[8192,128]{1,0:T(8,128)(2,1)}, bf16[512,128]{1,0:T(8,128)(2,1)}, bf16[8192,128]{1,0:T(8,128)(2,1)}) %tuple.58), branch_computations={%region_5.6_spmd, %region_6.10_spmd} | conditional | flops 2197814784 | bytes 65308752 | solution.py:77
  173.0 9.5 %fusion = (f32[512]{0:T(512)S(1)}, f32[512,8192]{1,0:T(8,128)}) fusion(pred[64,8192]{1,0:T(8,128)(4,1)S(1)} %get-tuple-element.80, bf16[512,128]{1,0:T(8,128)(2,1)S(1)} %get-tuple-element.81, bf16[8192,128]{1,0:T(8,128)(2,1)} %get-tuple-element.82), kind=kOutput, calls=%fused_computation.2 | convolution fusion | flops 1086324224 | bytes 19531776 | tf_op jit(solution)/shard_map/cond/branch_1_fun/dot_general | solution.py:46
  182.6 9.9 %multiply_reduce_fusion = f32[512]{0:T(512)S(1)} fusion(bf16[512,128]{1,0:T(8,128)(2,1)S(1)} %copy-done.10, bf16[8192,128]{1,0:T(8,128)(2,1)S(1)} %copy-done.6, f32[512,8192]{1,0:T(8,128)} %get-tuple-element.172, f32[512]{0:T(512)S(1)} %broadcast_maximum_fusion, pred[64,8192]{1,0:T(8,128)(4,1)S(1)} %get-tuple-element.80), kind=kOutput, calls=%fused_computation.3 | convolution fusion | flops 1094712832 | bytes 19533824 | tf_op jit(solution)/shard_map/cond/branch_1_fun/dot_general | solution.py:46
  192.5 8.5 %fusion.1 = f32[512]{0:T(512)S(1)} fusion(f32[512,8192]{1,0:T(8,128)} %get-tuple-element.172, f32[512]{0:T(512)S(1)} %broadcast_maximum_fusion, pred[64,8192]{1,0:T(8,128)(4,1)S(1)} %get-tuple-element.80), kind=kLoop, calls=%fused_computation.4 | loop fusion | flops 16776704 | bytes 17305600 | tf_op jit(solution)/shard_map/cond/branch_1_fun/reduce_sum | solution.py:72
  201.0 0.7 div.47
  201.7 0.7 max_broadcast_in_dim.21
  202.4 0.7 log.21
  203.1 38.1 %conditional.5 = (f32[512,128]{1,0:T(8,128)S(1)}, f32[8192,128]{1,0:T(8,128)}, f32[8192,128]{1,0:T(8,128)}) conditional(s32[]{:T(128)} %convert_element_type.36, () %tuple.56, (pred[64,8192]{1,0:T(8,128)(4,1)S(1)}, bf16[512,128]{1,0:T(8,128)(2,1)S(1)}, bf16[8192,128]{1,0:T(8,128)(2,1)}, f32[64,8]{1,0:T(8,128)}, f32[64,8]{1,0:T(8,128)}, ...), branch_computations={%region_10.11_spmd, %region_11.12_spmd} | conditional | flops 5398069760 | bytes 209471680 | solution.py:109
  203.6 0.8 sub.84
  204.4 0.8 add.23
  205.2 0.1 sub.81
  205.3 6.2 %exponential_select_fusion = f32[512,8192]{1,0:T(8,128)S(1)} fusion(bf16[512,128]{1,0:T(8,128)(2,1)S(1)} %get-tuple-element.86, bf16[8192,128]{1,0:T(8,128)(2,1)} %get-tuple-element.87, f32[512]{0:T(512)S(1)} %sub.81, pred[64,8192]{1,0:T(8,128)(4,1)S(1)} %get-tuple-element.85), kind=kOutput, calls=%fused_computation.7 | convolution fusion | flops 1086324736 | bytes 19531776 | tf_op jit(solution)/shard_map/cond/branch_1_fun/dot_general | solution.py:46
  211.5 5.7 %copy-done = f32[512,8192]{1,0:T(8,128)} copy-done((f32[512,8192]{1,0:T(8,128)}, f32[512,8192]{1,0:T(8,128)S(1)}, u32[]{:S(2)}) %copy-start) | copy-done | bytes 16777240 | tf_op jit(solution)/shard_map/cond
  217.2 4.3 fusion.2
  221.6 9.4 %multiply_convert_fusion = bf16[512,8192]{1,0:T(8,128)(2,1)} fusion(f32[512,8192]{1,0:T(8,128)} %copy-done, bf16[512,128]{1,0:T(8,128)(2,1)S(1)} %copy-done.11, bf16[8192,128]{1,0:T(8,128)(2,1)S(1)} %copy-done.7, f32[512]{0:T(512)S(1)} %sub.84), kind=kOutput, calls=%fused_computation.6 | convolution fusion | flops 1086324736 | bytes 27396096 | tf_op jit(solution)/shard_map/cond/branch_1_fun/dot_general | solution.py:46
  231.0 5.9 %fusion.23 = f32[512,128]{1,0:T(8,128)S(1)} fusion(bf16[512,8192]{1,0:T(8,128)(2,1)} %multiply_convert_fusion, bf16[8192,128]{1,0:T(8,128)(2,1)S(1)} %copy-done.4), kind=kOutput, calls=%fused_computation.67 | convolution fusion | flops 1073741824 | bytes 10747904 | tf_op jit(solution)/shard_map/cond/branch_1_fun/dot_general | solution.py:102
  236.8 4.4 fusion.24
  241.2 28.4 %conditional.6 = (f32[64,8]{1,0:T(8,128)S(1)}, f32[64,8]{1,0:T(8,128)S(1)}, f32[64,8]{1,0:T(8,128)S(1)}) conditional(s32[]{:T(128)} %convert_element_type.38, () %tuple.61, (pred[64,8192]{1,0:T(8,128)(4,1)S(1)}, bf16[512,128]{1,0:T(8,128)(2,1)S(1)}, bf16[8192,128]{1,0:T(8,128)(2,1)}, bf16[512,128]{1,0:T(8,128)(2,1)S(1)}, ...), branch_computations={%region_15.16_spmd, %region_16.20_spmd} | conditional | flops 2197814784 | bytes 64784436 | solution.py:77
  241.4 9.6 %fusion.4 = (f32[512]{0:T(512)S(1)}, f32[512,8192]{1,0:T(8,128)}) fusion(pred[64,8192]{1,0:T(8,128)(4,1)S(1)} %get-tuple-element.93, bf16[512,128]{1,0:T(8,128)(2,1)S(1)} %get-tuple-element.94, bf16[8192,128]{1,0:T(8,128)(2,1)} %get-tuple-element.95), kind=kOutput, calls=%fused_computation.12 | convolution fusion | flops 1086324224 | bytes 19531776 | tf_op jit(solution)/shard_map/cond/branch_1_fun/dot_general | solution.py:46
  250.9 9.9 %multiply_reduce_fusion.1 = f32[512]{0:T(512)S(1)} fusion(bf16[512,128]{1,0:T(8,128)(2,1)S(1)} %get-tuple-element.96, bf16[8192,128]{1,0:T(8,128)(2,1)S(1)} %copy-done.8, f32[512,8192]{1,0:T(8,128)} %get-tuple-element.176, f32[512]{0:T(512)S(1)} %broadcast_maximum_fusion.1, pred[64,8192]{1,0:T(8,128)(4,1)S(1)} %get-tuple-element.93), kind=kOutput, calls=%fused_computation.13 | convolution fusion | flops 1094712832 | bytes 19533824 | tf_op jit(solution)/shard_map/cond/branch_1_fun/dot_general | solution.py:46
  260.8 8.5 %fusion.5 = f32[512]{0:T(512)S(1)} fusion(f32[512,8192]{1,0:T(8,128)} %get-tuple-element.176, f32[512]{0:T(512)S(1)} %broadcast_maximum_fusion.1, pred[64,8192]{1,0:T(8,128)(4,1)S(1)} %get-tuple-element.93), kind=kLoop, calls=%fused_computation.14 | loop fusion | flops 16776704 | bytes 17305600 | tf_op jit(solution)/shard_map/cond/branch_1_fun/reduce_sum | solution.py:72
  269.3 0.1 div.49
  269.6 36.6 %conditional.7 = (f32[512,128]{1,0:T(8,128)S(1)}, f32[8192,128]{1,0:T(8,128)}, f32[8192,128]{1,0:T(8,128)}) conditional(s32[]{:T(128)} %convert_element_type.38, () %tuple.60, (pred[64,8192]{1,0:T(8,128)(4,1)S(1)}, bf16[512,128]{1,0:T(8,128)(2,1)S(1)}, bf16[8192,128]{1,0:T(8,128)(2,1)}, f32[64,8]{1,0:T(8,128)S(1)}, f32[64,8]{1,0:T(8,128)S(1)}, ...), branch_computations={%region_20.21_spmd, %region_21.22_spmd} | conditional | flops 5398069760 | bytes 208947360 | solution.py:109
  269.8 0.1 sub.92
  269.9 0.1 sub.89
  270.0 6.2 %exponential_select_fusion.1 = f32[512,8192]{1,0:T(8,128)S(1)} fusion(bf16[512,128]{1,0:T(8,128)(2,1)S(1)} %get-tuple-element.99, bf16[8192,128]{1,0:T(8,128)(2,1)} %get-tuple-element.100, f32[512]{0:T(512)S(1)} %sub.89, pred[64,8192]{1,0:T(8,128)(4,1)S(1)} %get-tuple-element.98), kind=kOutput, calls=%fused_computation.17 | convolution fusion | flops 1086324736 | bytes 19531776 | tf_op jit(solution)/shard_map/cond/branch_1_fun/dot_general | solution.py:46
  276.2 5.7 %copy-done.1 = f32[512,8192]{1,0:T(8,128)} copy-done((f32[512,8192]{1,0:T(8,128)}, f32[512,8192]{1,0:T(8,128)S(1)}, u32[]{:S(2)}) %copy-start.1) | copy-done | bytes 16777240 | tf_op jit(solution)/shard_map/cond
  281.9 4.4 fusion.6
  286.4 9.4 %multiply_convert_fusion.1 = bf16[512,8192]{1,0:T(8,128)(2,1)} fusion(f32[512,8192]{1,0:T(8,128)} %copy-done.1, bf16[512,128]{1,0:T(8,128)(2,1)S(1)} %get-tuple-element.103, bf16[8192,128]{1,0:T(8,128)(2,1)S(1)} %copy-done.9, f32[512]{0:T(512)S(1)} %sub.92), kind=kOutput, calls=%fused_computation.16 | convolution fusion | flops 1086324736 | bytes 27396096 | tf_op jit(solution)/shard_map/cond/branch_1_fun/dot_general | solution.py:46
  295.8 5.9 %fusion.25 = f32[512,128]{1,0:T(8,128)S(1)} fusion(bf16[512,8192]{1,0:T(8,128)(2,1)} %multiply_convert_fusion.1, bf16[8192,128]{1,0:T(8,128)(2,1)S(1)} %copy-done.5), kind=kOutput, calls=%fused_computation.69 | convolution fusion | flops 1073741824 | bytes 10747904 | tf_op jit(solution)/shard_map/cond/branch_1_fun/dot_general | solution.py:102
  301.6 4.3 fusion.26
  306.2 3.9 add.32
  310.1 3.9 add.31
  314.0 8.8 %pad_maximum_fusion = f32[8192,2,128]{2,1,0:T(2,128)} fusion(f32[8192,1,128]{2,1,0:T(1,128)S(1)} %bitcast.84, f32[8192,1,128]{2,1,0:T(1,128)S(1)} %bitcast.85), kind=kLoop, calls=%fused_computation.20 | loop fusion | flops 2097152 | bytes 16777216 | tf_op jit(solution)/shard_map/stack | solution.py:165
  322.8 0.6 copy-done.12
  323.4 0.6 dynamic-slice
  324.7 202.1 %all-reduce.3.cloned.1.call-done = f32[8192,2,128]{2,1,0:T(2,128)} async-done(((f32[8192,2,128]{2,1,0:T(2,128)}), f32[8192,2,128]{2,1,0:T(2,128)}) %all-reduce.3.cloned.1.call-update) | async-done | bytes 8388624
  526.8 1.0 dynamic-slice_convert_fusion
  527.8 0.5 broadcast.207
  528.3 0.8 reduce.14
  529.1 0.6 reshape.175
  529.7 4.2 all-to-all-start.3
  534.0 1.0 fusion.12
  535.0 0.8 reduce.13
  535.8 0.6 reshape.173
  536.4 3.0 all-to-all-done.3
  539.4 3.3 all-to-all-start.2
  542.7 0.7 pad_maximum_fusion.1
  543.5 0.6 copy.37
  544.1 4.0 all-to-all-done.2
  548.2 0.6 copy.36
  (47 shorter events, 0.7 us)
Async XLA Ops:
  7.2 88.1 %all-gather.3.cloned.1.call-start = ((), (), s32[]{:S(2)}) async-start(), calls=%async_computation.4 | async-start | bytes 2129920 | tf_op jit(solution)/shard_map/all_gather | solution.py:149
  17.6 155.4 %all-gather.5.cloned.1.call-start = ((), (), s32[]{:S(2)}) async-start(), calls=%async_computation.5 | async-start | bytes 2129920 | tf_op jit(solution)/shard_map/all_gather | solution.py:136
  26.9 499.9 %all-reduce.3.cloned.1.call-start = ((), (), s32[]{:S(2)}) async-start(), calls=%async_computation.6 | async-start | bytes 16777216
  173.0 9.6 %copy-start.6 = (bf16[8192,128]{1,0:T(8,128)(2,1)S(1)}, bf16[8192,128]{1,0:T(8,128)(2,1)}, u32[]{:S(2)}) copy-start(bf16[8192,128]{1,0:T(8,128)(2,1)} %get-tuple-element.84) | copy-start | bytes 6291460 | tf_op jit(solution)/shard_map/cond
  173.0 9.6 %copy-start.10 = (bf16[512,128]{1,0:T(8,128)(2,1)S(1)}, bf16[512,128]{1,0:T(8,128)(2,1)}, u32[]{:S(2)}) copy-start(bf16[512,128]{1,0:T(8,128)(2,1)} %get-tuple-element.83) | copy-start | bytes 393220 | tf_op jit(solution)/shard_map/cond
  205.3 11.9 %copy-start.11 = (bf16[512,128]{1,0:T(8,128)(2,1)S(1)}, bf16[512,128]{1,0:T(8,128)(2,1)}, u32[]{:S(2)}) copy-start(bf16[512,128]{1,0:T(8,128)(2,1)} %get-tuple-element.90) | copy-start | bytes 393220 | tf_op jit(solution)/shard_map/cond
  211.5 5.7 %copy-start = (f32[512,8192]{1,0:T(8,128)}, f32[512,8192]{1,0:T(8,128)S(1)}, u32[]{:S(2)}) copy-start(f32[512,8192]{1,0:T(8,128)S(1)} %exponential_select_fusion) | copy-start | bytes 50331652 | tf_op jit(solution)/shard_map/cond
  217.2 4.3 copy-start.7
  221.6 9.4 %copy-start.4 = (bf16[8192,128]{1,0:T(8,128)(2,1)S(1)}, bf16[8192,128]{1,0:T(8,128)(2,1)}, u32[]{:S(2)}) copy-start(bf16[8192,128]{1,0:T(8,128)(2,1)} %get-tuple-element.87) | copy-start | bytes 6291460 | tf_op jit(solution)/shard_map/cond
  231.0 5.9 %copy-start.2 = (bf16[512,8192]{1,0:T(8,128)(2,1)S(1)}, bf16[512,8192]{1,0:T(8,128)(2,1)}, u32[]{:S(2)}) copy-start(bf16[512,8192]{1,0:T(8,128)(2,1)} %multiply_convert_fusion) | copy-start | bytes 25165828 | tf_op jit(solution)/shard_map/cond
  241.4 9.6 %copy-start.8 = (bf16[8192,128]{1,0:T(8,128)(2,1)S(1)}, bf16[8192,128]{1,0:T(8,128)(2,1)}, u32[]{:S(2)}) copy-start(bf16[8192,128]{1,0:T(8,128)(2,1)} %get-tuple-element.97) | copy-start | bytes 6291460 | tf_op jit(solution)/shard_map/cond
  276.2 5.7 %copy-start.1 = (f32[512,8192]{1,0:T(8,128)}, f32[512,8192]{1,0:T(8,128)S(1)}, u32[]{:S(2)}) copy-start(f32[512,8192]{1,0:T(8,128)S(1)} %exponential_select_fusion.1) | copy-start | bytes 50331652 | tf_op jit(solution)/shard_map/cond
  281.9 4.4 copy-start.9
  286.4 9.4 %copy-start.5 = (bf16[8192,128]{1,0:T(8,128)(2,1)S(1)}, bf16[8192,128]{1,0:T(8,128)(2,1)}, u32[]{:S(2)}) copy-start(bf16[8192,128]{1,0:T(8,128)(2,1)} %get-tuple-element.100) | copy-start | bytes 6291460 | tf_op jit(solution)/shard_map/cond
  295.8 5.9 %copy-start.3 = (bf16[512,8192]{1,0:T(8,128)(2,1)S(1)}, bf16[512,8192]{1,0:T(8,128)(2,1)}, u32[]{:S(2)}) copy-start(bf16[512,8192]{1,0:T(8,128)(2,1)} %multiply_convert_fusion.1) | copy-start | bytes 25165828 | tf_op jit(solution)/shard_map/cond
  322.7 0.7 copy-start.12
  529.7 9.7 %all-to-all-start.3 = ((bf16[4,2,2048]{2,1,0:T(2,128)(2,1)}), bf16[4,2,2048]{2,1,0:T(2,128)(2,1)S(1)}, u32[]{:S(2)}, u32[]{:S(2)}) async-start(bf16[4,2,2048]{2,1,0:T(2,128)(2,1)} %reshape.175), calls=%async_computation.3 | async-start | bytes 65536 | tf_op jit(solution)/shard_map/all_to_all | solution.py:177
  539.4 8.7 %all-to-all-start.2 = ((bf16[4,2,2048]{2,1,0:T(2,128)(2,1)}), bf16[4,2,2048]{2,1,0:T(2,128)(2,1)S(1)}, u32[]{:S(2)}, u32[]{:S(2)}) async-start(bf16[4,2,2048]{2,1,0:T(2,128)(2,1)} %reshape.173), calls=%async_computation.2 | async-start | bytes 65536 | tf_op jit(solution)/shard_map/all_to_all | solution.py:176
Sparse Core Ops, SparseCore 0:
  17.8 77.4 all-gather.2
  98.0 74.9 all-gather.4
  322.9 203.8 all-reduce.2
where the time goes:
time: 564 us; the launch traced here: 556 us
  waiting for transfers between devices  347 us (62%)
  matrix products  99.2 us (18%)
  other arithmetic  42 us (7%)
  local copies, waits for them, and re-layouts  24.3 us (4%)
  blocking collectives  18.1 us (3%)
  between operations  16.1 us (3%)
  starting transfers between devices  7.63 us (1%)
    unnamed x4, waiting for transfers between devices  202 us
    all_gather x1, waiting for transfers between devices, body(): lax.all_gather(values, 'ctx', axis=0, tiled=True)  77.8 us
    dot_general x8, matrix products, contract_rows(): lax.dot_general(left, right, (((1,), (1,)), ((), ())), preferred_element_...  70.1 us
    all_gather x1, waiting for transfers between devices, body(): lax.all_gather(keys, 'ctx', axis=0, tiled=True)  60.1 us
    dot_general x4, matrix products, contract_first(): lax.dot_general(left, right, (((0,), (0,)), ((), ())), preferred_element_...  17.4 us
    reduce_sum x2, other arithmetic, stats_compute(): return (new_high, jnp.sum(probs, axis=2), jnp.sum(probs * d_probs, axis=2))  17 us
    dot_general x2, matrix products, grad_compute(): grad_rows = jnp.dot(d_scores, keys, preferred_element_type=jnp.float32)  11.7 us
    cond x24, local copies, waits for them, and re-layouts  11.4 us
  transfers between devices with their start and end apart: 5, of which 5 were waited for; matrix products, arithmetic and copies ran while one was open for 2% of the time, Pallas kernels for 0%

commit v1 on v0

--- a/solution.py
+++ b/solution.py
@@ -133,7 +133,9 @@
     )
     piece = (
         lax.all_gather(keys, "ctx", axis=0, tiled=True),
-        lax.all_gather(values, "ctx", axis=0, tiled=True),
+        jnp.concatenate(
+            lax.all_to_all(jnp.stack([values] * lax.axis_size("ctx")), "ctx", 0, 0), axis=0
+        ),
     )
     stats = tuple(
         (

time: 564 us -> 539 us (0.956)
  waiting for transfers between devices: 347 us -> 311 us
  starting transfers between devices: 7.63 us -> 19.9 us
    all_gather x1, waiting for transfers between devices: 77.8 us -> 49.6 us  [body(): lax.all_gather(values, 'ctx', axis=0, tiled=True)]
    all_to_all x0 -> x1, starting transfers between devices: none -> 12.3 us  [body(): lax.all_to_all(jnp.stack([values] * lax.axis_size('ctx')), 'ctx', 0, 0)]
    all_gather x1, waiting for transfers between devices: 60.1 us -> 51.5 us  [body(): lax.all_gather(keys, 'ctx', axis=0, tiled=True)]
    cond x24 -> x18, local copies, waits for them, and re-layouts: 11.4 us -> 11.4 us
  transfers between devices with their start and end apart: 5 -> 6, of which waited for: 5 -> 5; matrix products, arithmetic and copies ran while one was open for 2% -> 8% of each run, Pallas kernels for 0% -> 0%
where the time goes in v1:
time: 539 us; the launch traced here: 530 us
  waiting for transfers between devices  311 us (58%)
  matrix products  100 us (19%)
  other arithmetic  41.3 us (8%)
  local copies, waits for them, and re-layouts  22.8 us (4%)
  starting transfers between devices  19.9 us (4%)
  blocking collectives  17.4 us (3%)
  between operations  16.1 us (3%)
    unnamed x4, waiting for transfers between devices  203 us
    dot_general x8, matrix products, contract_rows(): lax.dot_general(left, right, (((1,), (1,)), ((), ())), preferred_element_...  71.1 us
    all_gather x1, waiting for transfers between devices, body(): lax.all_gather(keys, 'ctx', axis=0, tiled=True)  51.5 us
    all_gather x1, waiting for transfers between devices, body(): lax.all_gather(values, 'ctx', axis=0, tiled=True)  49.6 us
    dot_general x4, matrix products, contract_first(): lax.dot_general(left, right, (((0,), (0,)), ((), ())), preferred_element_...  17.4 us
    reduce_sum x2, other arithmetic, stats_compute(): return (new_high, jnp.sum(probs, axis=2), jnp.sum(probs * d_probs, axis=2))  17 us
    all_to_all x1, starting transfers between devices, body(): lax.all_to_all(jnp.stack([values] * lax.axis_size('ctx')), 'ctx', 0, 0)  12.3 us
    dot_general x2, matrix products, grad_compute(): grad_rows = jnp.dot(d_scores, keys, preferred_element_type=jnp.float32)  11.7 us
  transfers between devices with their start and end apart: 6, of which 5 were waited for; matrix products, arithmetic and copies ran while one was open for 8% of the time, Pallas kernels for 0%

profile of v1, /device:TPU:8, one launch (start us, length us, event | category | flops | bytes accessed | tf_op | source)
XLA Modules:
  0.0 530.1 jit_solution(4763304610498905523)
XLA Ops:
  7.2 0.8 copy.34
  8.0 9.6 %all_to_all.71 = bf16[32,4,128]{2,0,1:T(8,128)(2,1)} all-to-all(bf16[32,4,128]{2,0,1:T(8,128)(2,1)S(1)} %copy.34), channel_id=1, replica_groups=mesh['ctx'=64,'head'=4] {'head'}, dimensions={1} | all-to-all | bytes 65536 | tf_op jit(solution)/shard_map/all_to_all | solution.py:114
  17.6 0.8 copy.35
  18.4 7.8 %all_to_all.72 = bf16[32,4,128]{2,0,1:T(8,128)(2,1)S(1)} all-to-all(bf16[32,4,128]{2,0,1:T(8,128)(2,1)S(1)} %copy.35), channel_id=1, replica_groups=mesh['ctx'=64,'head'=4] {'head'}, dimensions={1} | all-to-all | bytes 65536 | tf_op jit(solution)/shard_map/all_to_all | solution.py:115
  26.2 1.8 stack.12
  28.0 12.3 %all-to-all-start.2 = ((bf16[64,128,128]{2,1,0:T(8,128)(2,1)}), bf16[64,128,128]{2,1,0:T(8,128)(2,1)}, u32[]{:S(2)}, u32[]{:S(2)}) async-start(bf16[64,128,128]{2,1,0:T(8,128)(2,1)} %stack.12), calls=%async_computation.2 | async-start | bytes 4194304 | tf_op jit(solution)/shard_map/all_to_all | solution.py:137
  40.4 0.7 all-gather.5.cloned.1.call-update
  41.1 0.7 copy.33
  41.9 0.1 reduce.12
  42.0 0.7 sub.100
  42.8 0.7 select_reduce_fusion.3
  43.5 0.3 select_reduce_fusion
  43.9 2.3 fusion.16
  47.5 1.1 slice_bitcast_fusion.2
  48.6 51.5 %all-gather.3.cloned.1.call-done = bf16[8192,128]{1,0:T(8,128)(2,1)} async-done(((bf16[128,128]{1,0:T(8,128)(2,1)}), bf16[8192,128]{1,0:T(8,128)(2,1)}) %all-gather.3.cloned.1.call-update) | async-done | bytes 2097168 | tf_op jit(solution)/shard_map/all_gather | solution.py:151
  100.2 28.6 %conditional.6 = (f32[64,8]{1,0:T(8,128)S(1)}, f32[64,8]{1,0:T(8,128)S(1)}, f32[64,8]{1,0:T(8,128)S(1)}) conditional(s32[]{:T(128)} %convert_element_type.38, () %tuple.61, (pred[64,8192]{1,0:T(8,128)(4,1)S(1)}, bf16[512,128]{1,0:T(8,128)(2,1)S(1)}, bf16[8192,128]{1,0:T(8,128)(2,1)}, bf16[512,128]{1,0:T(8,128)(2,1)S(1)}, ...), branch_computations={%region_15.16_spmd, %region_16.20_spmd} | conditional | flops 2197814784 | bytes 56395800 | solution.py:77
  100.2 9.4 %fusion.4 = (f32[512]{0:T(512)S(1)}, f32[512,8192]{1,0:T(8,128)}) fusion(pred[64,8192]{1,0:T(8,128)(4,1)S(1)} %get-tuple-element.93, bf16[512,128]{1,0:T(8,128)(2,1)S(1)} %get-tuple-element.94, bf16[8192,128]{1,0:T(8,128)(2,1)} %get-tuple-element.95), kind=kOutput, calls=%fused_computation.12 | convolution fusion | flops 1086324224 | bytes 19531776 | tf_op jit(solution)/shard_map/cond/branch_1_fun/dot_general | solution.py:46
  109.6 10.5 %multiply_reduce_fusion.1 = f32[512]{0:T(512)S(1)} fusion(bf16[512,128]{1,0:T(8,128)(2,1)S(1)} %get-tuple-element.96, bf16[8192,128]{1,0:T(8,128)(2,1)} %get-tuple-element.97, f32[512,8192]{1,0:T(8,128)} %get-tuple-element.176, f32[512]{0:T(512)S(1)} %broadcast_maximum_fusion.1, pred[64,8192]{1,0:T(8,128)(4,1)S(1)} %get-tuple-element.93), kind=kOutput, calls=%fused_computation.13 | convolution fusion | flops 1094712832 | bytes 19533824 | tf_op jit(solution)/shard_map/cond/branch_1_fun/dot_general | solution.py:46
  120.0 8.5 %fusion.5 = f32[512]{0:T(512)S(1)} fusion(f32[512,8192]{1,0:T(8,128)} %get-tuple-element.176, f32[512]{0:T(512)S(1)} %broadcast_maximum_fusion.1, pred[64,8192]{1,0:T(8,128)(4,1)S(1)} %get-tuple-element.93), kind=kLoop, calls=%fused_computation.14 | loop fusion | flops 16776704 | bytes 17305600 | tf_op jit(solution)/shard_map/cond/branch_1_fun/reduce_sum | solution.py:72
  128.5 0.1 div.49
  128.8 49.6 %all-gather.5.cloned.1.call-done = bf16[8192,128]{1,0:T(8,128)(2,1)} async-done(((bf16[128,128]{1,0:T(8,128)(2,1)}), bf16[8192,128]{1,0:T(8,128)(2,1)}) %all-gather.5.cloned.1.call-update) | async-done | bytes 2097168 | tf_op jit(solution)/shard_map/all_gather | solution.py:152
  178.4 36.9 %conditional.7 = (f32[512,128]{1,0:T(8,128)S(1)}, f32[8192,128]{1,0:T(8,128)}, f32[8192,128]{1,0:T(8,128)}) conditional(s32[]{:T(128)} %convert_element_type.38, () %tuple.60, (pred[64,8192]{1,0:T(8,128)(4,1)S(1)}, bf16[512,128]{1,0:T(8,128)(2,1)S(1)}, bf16[8192,128]{1,0:T(8,128)(2,1)}, f32[64,8]{1,0:T(8,128)S(1)}, f32[64,8]{1,0:T(8,128)S(1)}, ...), branch_computations={%region_20.21_spmd, %region_21.22_spmd} | conditional | flops 5398069760 | bytes 209471680 | solution.py:109
  179.0 0.1 sub.92
  179.1 0.1 sub.89
  179.2 6.2 %exponential_select_fusion.1 = f32[512,8192]{1,0:T(8,128)S(1)} fusion(bf16[512,128]{1,0:T(8,128)(2,1)S(1)} %get-tuple-element.99, bf16[8192,128]{1,0:T(8,128)(2,1)} %get-tuple-element.100, f32[512]{0:T(512)S(1)} %sub.89, pred[64,8192]{1,0:T(8,128)(4,1)S(1)} %get-tuple-element.98), kind=kOutput, calls=%fused_computation.17 | convolution fusion | flops 1086324736 | bytes 19531776 | tf_op jit(solution)/shard_map/cond/branch_1_fun/dot_general | solution.py:46
  185.4 5.7 %copy-done = f32[512,8192]{1,0:T(8,128)} copy-done((f32[512,8192]{1,0:T(8,128)}, f32[512,8192]{1,0:T(8,128)S(1)}, u32[]{:S(2)}) %copy-start) | copy-done | bytes 16777240 | tf_op jit(solution)/shard_map/cond
  191.1 4.4 fusion.6
  195.5 9.6 %multiply_convert_fusion.1 = bf16[512,8192]{1,0:T(8,128)(2,1)} fusion(f32[512,8192]{1,0:T(8,128)} %copy-done, bf16[512,128]{1,0:T(8,128)(2,1)} %copy-done.8, bf16[8192,128]{1,0:T(8,128)(2,1)S(1)} %copy-done.6, f32[512]{0:T(512)S(1)} %sub.92), kind=kOutput, calls=%fused_computation.16 | convolution fusion | flops 1086324736 | bytes 27396096 | tf_op jit(solution)/shard_map/cond/branch_1_fun/dot_general | solution.py:46
  205.1 5.9 %fusion.25 = f32[512,128]{1,0:T(8,128)S(1)} fusion(bf16[512,8192]{1,0:T(8,128)(2,1)} %multiply_convert_fusion.1, bf16[8192,128]{1,0:T(8,128)(2,1)S(1)} %copy-done.4), kind=kOutput, calls=%fused_computation.69 | convolution fusion | flops 1073741824 | bytes 10747904 | tf_op jit(solution)/shard_map/cond/branch_1_fun/dot_general | solution.py:102
  211.0 4.3 fusion.26
  215.3 28.8 %conditional.4 = (f32[64,8]{1,0:T(8,128)S(1)}, f32[64,8]{1,0:T(8,128)S(1)}, f32[64,8]{1,0:T(8,128)S(1)}) conditional(s32[]{:T(128)} %convert_element_type.36, () %tuple.57, (pred[64,8192]{1,0:T(8,128)(4,1)S(1)}, bf16[512,128]{1,0:T(8,128)(2,1)S(1)}, bf16[8192,128]{1,0:T(8,128)(2,1)}, bf16[512,128]{1,0:T(8,128)(2,1)S(1)}, ...), branch_computations={%region_5.6_spmd, %region_6.10_spmd} | conditional | flops 2197814784 | bytes 56395800 | solution.py:77
  215.5 9.4 %fusion = (f32[512]{0:T(512)S(1)}, f32[512,8192]{1,0:T(8,128)}) fusion(pred[64,8192]{1,0:T(8,128)(4,1)S(1)} %get-tuple-element.80, bf16[512,128]{1,0:T(8,128)(2,1)S(1)} %get-tuple-element.81, bf16[8192,128]{1,0:T(8,128)(2,1)} %get-tuple-element.82), kind=kOutput, calls=%fused_computation.2 | convolution fusion | flops 1086324224 | bytes 19531776 | tf_op jit(solution)/shard_map/cond/branch_1_fun/dot_general | solution.py:46
  224.9 10.5 %multiply_reduce_fusion = f32[512]{0:T(512)S(1)} fusion(bf16[512,128]{1,0:T(8,128)(2,1)S(1)} %get-tuple-element.83, bf16[8192,128]{1,0:T(8,128)(2,1)} %get-tuple-element.84, f32[512,8192]{1,0:T(8,128)} %get-tuple-element.172, f32[512]{0:T(512)S(1)} %broadcast_maximum_fusion, pred[64,8192]{1,0:T(8,128)(4,1)S(1)} %get-tuple-element.80), kind=kOutput, calls=%fused_computation.3 | convolution fusion | flops 1094712832 | bytes 19533824 | tf_op jit(solution)/shard_map/cond/branch_1_fun/dot_general | solution.py:46
  235.4 8.5 %fusion.1 = f32[512]{0:T(512)S(1)} fusion(f32[512,8192]{1,0:T(8,128)} %get-tuple-element.172, f32[512]{0:T(512)S(1)} %broadcast_maximum_fusion, pred[64,8192]{1,0:T(8,128)(4,1)S(1)} %get-tuple-element.80), kind=kLoop, calls=%fused_computation.4 | loop fusion | flops 16776704 | bytes 17305600 | tf_op jit(solution)/shard_map/cond/branch_1_fun/reduce_sum | solution.py:72
  243.9 0.1 div.47
  244.1 36.5 %conditional.5 = (f32[512,128]{1,0:T(8,128)S(1)}, f32[8192,128]{1,0:T(8,128)}, f32[8192,128]{1,0:T(8,128)}) conditional(s32[]{:T(128)} %convert_element_type.36, () %tuple.56, (pred[64,8192]{1,0:T(8,128)(4,1)S(1)}, bf16[512,128]{1,0:T(8,128)(2,1)S(1)}, bf16[8192,128]{1,0:T(8,128)(2,1)}, f32[64,8]{1,0:T(8,128)S(1)}, f32[64,8]{1,0:T(8,128)S(1)}, ...), branch_computations={%region_10.11_spmd, %region_11.12_spmd} | conditional | flops 5398069760 | bytes 208947360 | solution.py:109
  244.4 0.1 sub.84
  244.5 0.1 sub.81
  244.6 6.2 %exponential_select_fusion = f32[512,8192]{1,0:T(8,128)S(1)} fusion(bf16[512,128]{1,0:T(8,128)(2,1)S(1)} %get-tuple-element.86, bf16[8192,128]{1,0:T(8,128)(2,1)} %get-tuple-element.87, f32[512]{0:T(512)S(1)} %sub.81, pred[64,8192]{1,0:T(8,128)(4,1)S(1)} %get-tuple-element.85), kind=kOutput, calls=%fused_computation.7 | convolution fusion | flops 1086324736 | bytes 19531776 | tf_op jit(solution)/shard_map/cond/branch_1_fun/dot_general | solution.py:46
  250.7 5.7 %copy-done.1 = f32[512,8192]{1,0:T(8,128)} copy-done((f32[512,8192]{1,0:T(8,128)}, f32[512,8192]{1,0:T(8,128)S(1)}, u32[]{:S(2)}) %copy-start.1) | copy-done | bytes 16777240 | tf_op jit(solution)/shard_map/cond
  256.5 4.4 fusion.2
  260.8 9.4 %multiply_convert_fusion = bf16[512,8192]{1,0:T(8,128)(2,1)} fusion(f32[512,8192]{1,0:T(8,128)} %copy-done.1, bf16[512,128]{1,0:T(8,128)(2,1)S(1)} %get-tuple-element.90, bf16[8192,128]{1,0:T(8,128)(2,1)S(1)} %copy-done.7, f32[512]{0:T(512)S(1)} %sub.84), kind=kOutput, calls=%fused_computation.6 | convolution fusion | flops 1086324736 | bytes 27396096 | tf_op jit(solution)/shard_map/cond/branch_1_fun/dot_general | solution.py:46
  270.3 5.9 %fusion.23 = f32[512,128]{1,0:T(8,128)S(1)} fusion(bf16[512,8192]{1,0:T(8,128)(2,1)} %multiply_convert_fusion, bf16[8192,128]{1,0:T(8,128)(2,1)S(1)} %copy-done.5), kind=kOutput, calls=%fused_computation.67 | convolution fusion | flops 1073741824 | bytes 10747904 | tf_op jit(solution)/shard_map/cond/branch_1_fun/dot_general | solution.py:102
  276.1 4.3 fusion.24
  280.7 3.9 add.32
  284.6 3.9 add.31
  288.5 8.8 %pad_maximum_fusion = f32[8192,2,128]{2,1,0:T(2,128)} fusion(f32[8192,1,128]{2,1,0:T(1,128)S(1)} %bitcast.85, f32[8192,1,128]{2,1,0:T(1,128)S(1)} %bitcast.86), kind=kLoop, calls=%fused_computation.20 | loop fusion | flops 2097152 | bytes 16777216 | tf_op jit(solution)/shard_map/stack | solution.py:167
  297.3 0.6 copy-done.10
  297.9 0.6 dynamic-slice
  299.2 202.1 %all-reduce.3.cloned.1.call-done = f32[8192,2,128]{2,1,0:T(2,128)} async-done(((f32[8192,2,128]{2,1,0:T(2,128)}), f32[8192,2,128]{2,1,0:T(2,128)}) %all-reduce.3.cloned.1.call-update) | async-done | bytes 8388624
  501.3 1.0 dynamic-slice_convert_fusion
  502.3 0.5 broadcast.208
  502.8 0.8 reduce.14
  503.6 0.6 reshape.182
  504.3 4.2 all-to-all-start.4
  508.5 1.0 fusion.12
  509.5 0.8 reduce.13
  510.3 0.6 reshape.180
  510.9 3.0 all-to-all-done.4
  514.0 3.3 all-to-all-start.3
  517.2 0.7 pad_maximum_fusion.1
  518.0 0.6 copy.37
  518.6 4.0 all-to-all-done.3
  522.7 0.6 copy.36
  (46 shorter events, 0.9 us)
Async XLA Ops:
  7.2 93.0 %all-gather.3.cloned.1.call-start = ((), (), s32[]{:S(2)}) async-start(), calls=%async_computation.5 | async-start | bytes 2129920 | tf_op jit(solution)/shard_map/all_gather | solution.py:151
  26.2 14.2 %copy-start.9 = (bf16[32,4,128]{2,0,1:T(8,128)(2,1)}, bf16[32,4,128]{2,0,1:T(8,128)(2,1)S(1)}, u32[]{:S(2)}) copy-start(bf16[32,4,128]{2,0,1:T(8,128)(2,1)S(1)} %all_to_all.72) | copy-start | bytes 98308
  28.0 72.2 %all-to-all-start.2 = ((bf16[64,128,128]{2,1,0:T(8,128)(2,1)}), bf16[64,128,128]{2,1,0:T(8,128)(2,1)}, u32[]{:S(2)}, u32[]{:S(2)}) async-start(bf16[64,128,128]{2,1,0:T(8,128)(2,1)} %stack.12), calls=%async_computation.2 | async-start | bytes 4194304 | tf_op jit(solution)/shard_map/all_to_all | solution.py:137
  40.3 138.1 %all-gather.5.cloned.1.call-start = ((), (), s32[]{:S(2)}) async-start(), calls=%async_computation.6 | async-start | bytes 2129920 | tf_op jit(solution)/shard_map/all_gather | solution.py:152
  41.1 460.3 %all-reduce.3.cloned.1.call-start = ((), (), s32[]{:S(2)}) async-start(), calls=%async_computation.7 | async-start | bytes 16777216
  179.0 6.4 %copy-start.8 = (bf16[512,128]{1,0:T(8,128)(2,1)}, bf16[512,128]{1,0:T(8,128)(2,1)S(1)}, u32[]{:S(2)}) copy-start(bf16[512,128]{1,0:T(8,128)(2,1)S(1)} %get-tuple-element.103) | copy-start | bytes 393220 | tf_op jit(solution)/shard_map/cond
  185.3 5.7 %copy-start = (f32[512,8192]{1,0:T(8,128)}, f32[512,8192]{1,0:T(8,128)S(1)}, u32[]{:S(2)}) copy-start(f32[512,8192]{1,0:T(8,128)S(1)} %exponential_select_fusion.1) | copy-start | bytes 50331652 | tf_op jit(solution)/shard_map/cond
  191.1 4.4 copy-start.6
  195.5 9.6 %copy-start.4 = (bf16[8192,128]{1,0:T(8,128)(2,1)S(1)}, bf16[8192,128]{1,0:T(8,128)(2,1)}, u32[]{:S(2)}) copy-start(bf16[8192,128]{1,0:T(8,128)(2,1)} %get-tuple-element.100) | copy-start | bytes 6291460 | tf_op jit(solution)/shard_map/cond
  205.1 5.9 %copy-start.2 = (bf16[512,8192]{1,0:T(8,128)(2,1)S(1)}, bf16[512,8192]{1,0:T(8,128)(2,1)}, u32[]{:S(2)}) copy-start(bf16[512,8192]{1,0:T(8,128)(2,1)} %multiply_convert_fusion.1) | copy-start | bytes 25165828 | tf_op jit(solution)/shard_map/cond
  250.7 5.7 %copy-start.1 = (f32[512,8192]{1,0:T(8,128)}, f32[512,8192]{1,0:T(8,128)S(1)}, u32[]{:S(2)}) copy-start(f32[512,8192]{1,0:T(8,128)S(1)} %exponential_select_fusion) | copy-start | bytes 50331652 | tf_op jit(solution)/shard_map/cond
  256.5 4.4 copy-start.7
  260.8 9.4 %copy-start.5 = (bf16[8192,128]{1,0:T(8,128)(2,1)S(1)}, bf16[8192,128]{1,0:T(8,128)(2,1)}, u32[]{:S(2)}) copy-start(bf16[8192,128]{1,0:T(8,128)(2,1)} %get-tuple-element.87) | copy-start | bytes 6291460 | tf_op jit(solution)/shard_map/cond
  270.3 5.9 %copy-start.3 = (bf16[512,8192]{1,0:T(8,128)(2,1)S(1)}, bf16[512,8192]{1,0:T(8,128)(2,1)}, u32[]{:S(2)}) copy-start(bf16[512,8192]{1,0:T(8,128)(2,1)} %multiply_convert_fusion) | copy-start | bytes 25165828 | tf_op jit(solution)/shard_map/cond
  297.2 0.7 copy-start.10
  504.3 9.7 %all-to-all-start.4 = ((bf16[4,2,2048]{2,1,0:T(2,128)(2,1)}), bf16[4,2,2048]{2,1,0:T(2,128)(2,1)S(1)}, u32[]{:S(2)}, u32[]{:S(2)}) async-start(bf16[4,2,2048]{2,1,0:T(2,128)(2,1)} %reshape.182), calls=%async_computation.4 | async-start | bytes 65536 | tf_op jit(solution)/shard_map/all_to_all | solution.py:179
  514.0 8.7 %all-to-all-start.3 = ((bf16[4,2,2048]{2,1,0:T(2,128)(2,1)}), bf16[4,2,2048]{2,1,0:T(2,128)(2,1)S(1)}, u32[]{:S(2)}, u32[]{:S(2)}) async-start(bf16[4,2,2048]{2,1,0:T(2,128)(2,1)} %reshape.180), calls=%async_computation.3 | async-start | bytes 65536 | tf_op jit(solution)/shard_map/all_to_all | solution.py:178
Sparse Core Ops, SparseCore 0:
  17.8 82.3 all-gather.2
  103.5 74.8 all-gather.4
  297.4 203.8 all-reduce.2
